TPU v7x, 32 devices: a whole 2x2x4 slice. The times are simulated.
32 devices in a mesh: dp: 8 (over z, x), head: 4 (over y, core).
Axes of the slice: x: 2, y: 2, z: 4, core: 2. Of those that a mesh axis runs over, the one named last changes fastest.
Arguments:
- input_segments: float32 [16384, 32], P(('dp', 'head')), may hold values from -6 to 6
- filler_flags: int32 [16384, 32], P(('dp', 'head')), may hold values 0 or 1
- sequence_owner: int32 [16384], P(('dp', 'head')), may hold values from 0 to 127, never falling along the last dimension, each value on 1 to 256 neighbouring positions
- prediction_adjoint: bfloat16 [16384, 1280], P('dp', 'head'), may hold values from -6 to 6
- quadratic_params: float32 [6, 1280, 1280], P(None, ('dp', 'head')), may hold values from -0.3354102 to 0.3354102, as said below
- quadratic_velocity: float32 [6, 1280, 1280], P(None, ('dp', 'head')), may hold values from -384 to 384
- quadratic_mean: float32 [6, 1280, 1280], P(None, ('dp', 'head')), may hold values from -0.15625 to 0.15625
- perceptron_params: float32 [2, 1280, 5120], P(None, ('dp', 'head')), may hold values from -0.15625 to 0.15625
- perceptron_velocity: float32 [2, 1280, 5120], P(None, ('dp', 'head')), may hold values from -384 to 384
- perceptron_mean: float32 [2, 1280, 5120], P(None, ('dp', 'head')), may hold values from -0.15625 to 0.15625
- embedder_params: float32 [2, 1280, 64], P(None, ('dp', 'head')), may hold values from -0.75 to 0.75
- embedder_velocity: float32 [2, 1280, 64], P(None, ('dp', 'head')), may hold values from -384 to 384
- embedder_mean: float32 [2, 1280, 64], P(None, ('dp', 'head')), may hold values from -0.75 to 0.75
- bias_gain_params: float32 [5, 1280], P(None, ('dp', 'head')), may hold values from -1.6 to 1.6, as said below
- bias_gain_velocity: float32 [5, 1280], P(None, ('dp', 'head')), may hold values from -384 to 384
- bias_gain_mean: float32 [5, 1280], P(None, ('dp', 'head')), may hold values from -1.6 to 1.6, as said below
- readout_params: float32 [2, 1280, 1280], P(None, 'dp', 'head'), may hold values from -0.15625 to 0.15625
- readout_velocity: float32 [2, 1280, 1280], P(None, 'dp', 'head'), may hold values from -384 to 384
- readout_mean: float32 [2, 1280, 1280], P(None, 'dp', 'head'), may hold values from -0.15625 to 0.15625
Outputs:
- prediction: bfloat16 [16384, 1280], P('dp', 'head')
- segment_derivative: float32 [16384, 32], P(('dp', 'head'))
- quadratic_params_fresh: float32 [6, 1280, 1280], P(None, ('dp', 'head'))
- quadratic_velocity_fresh: float32 [6, 1280, 1280], P(None, ('dp', 'head'))
- quadratic_mean_fresh: float32 [6, 1280, 1280], P(None, ('dp', 'head'))
- perceptron_params_fresh: float32 [2, 1280, 5120], P(None, ('dp', 'head'))
- perceptron_velocity_fresh: float32 [2, 1280, 5120], P(None, ('dp', 'head'))
- perceptron_mean_fresh: float32 [2, 1280, 5120], P(None, ('dp', 'head'))
- embedder_params_fresh: float32 [2, 1280, 64], P(None, ('dp', 'head'))
- embedder_velocity_fresh: float32 [2, 1280, 64], P(None, ('dp', 'head'))
- embedder_mean_fresh: float32 [2, 1280, 64], P(None, ('dp', 'head'))
- bias_gain_params_fresh: float32 [5, 1280], P(None, ('dp', 'head'))
- bias_gain_velocity_fresh: float32 [5, 1280], P(None, ('dp', 'head'))
- bias_gain_mean_fresh: float32 [5, 1280], P(None, ('dp', 'head'))
- readout_params_fresh: float32 [2, 1280, 1280], P(None, 'dp', 'head')
- readout_velocity_fresh: float32 [2, 1280, 1280], P(None, 'dp', 'head')
- readout_mean_fresh: float32 [2, 1280, 1280], P(None, 'dp', 'head')
Inputs may be any that keep to these rules, and one draw needn't show every extreme that they name: quadratic_params entries lie within this range. bias_gain_params entries lie within this range. bias_gain_mean entries lie within this range.
All inputs are finite; a program needn't handle non-finite values. No bound on the sum of `filler_flags` on one device may be relied on, other than what follows from the above.
Results may differ from a plain program's by a relative error of at most 0.019.
Values may be sent and summed in bfloat16 or wider, within the bound.
A program may use at most 448 MiB of HBM per device.

v0:
```python
import jax
import jax.numpy as jnp
from jax import lax
from jax.sharding import PartitionSpec as P

D = 1280
HEADS = 16
HEAD_DIM = 80
PATCH = 32
SEQ = 512
EPSILON = 1e-06
MOMENTUM = 0.9
AVG_DECAY = 0.9


def matrix_multiply(left_mat, right_mat):
    return jnp.dot(left_mat, right_mat, preferred_element_type=jnp.float32)


def flipped_bilinear(left_mat, right_mat):
    return lax.dot_general(
        left_mat, right_mat, (((1,), (1,)), ((), ())), preferred_element_type=jnp.float32
    )


def bilinear_flipped(left_mat, right_mat):
    return lax.dot_general(
        left_mat, right_mat, (((0,), (0,)), ((), ())), preferred_element_type=jnp.float32
    )


def rounded(values_in):
    return values_in.astype(jnp.bfloat16)


def rms_gain(values_in, gains_in):
    return (
        values_in
        * lax.rsqrt(jnp.mean(values_in * values_in, axis=-1, keepdims=True) + EPSILON)
        * gains_in
    )


def silu_slope(values_in):
    logistic = jax.nn.sigmoid(values_in)
    return logistic * (1.0 + values_in * (1.0 - logistic))


def rope_tables():
    half_dim = HEAD_DIM // 2
    position = jnp.arange(SEQ, dtype=jnp.float32)[:, None]
    spacing = 10000.0 ** (-jnp.arange(half_dim, dtype=jnp.float32) / half_dim)
    angles = position * spacing[None, :]
    return (jnp.cos(angles), jnp.sin(angles))


def rotate(heads_in, cosines, sines):
    half_dim = heads_in.shape[-1] // 2
    lower_half = heads_in[..., :half_dim]
    upper_half = heads_in[..., half_dim:]
    cos_rows = cosines[:, None, :]
    sin_rows = sines[:, None, :]
    return jnp.concatenate(
        [
            lower_half * cos_rows - upper_half * sin_rows,
            upper_half * cos_rows + lower_half * sin_rows,
        ],
        axis=-1,
    )


def masked_scores(query_heads, key_heads, segments):
    scores = jnp.einsum(
        "qhd,khd->hqk", query_heads, key_heads, preferred_element_type=jnp.float32
    ) * HEAD_DIM ** (-0.5)
    places = jnp.arange(SEQ)
    allowed = (places[:, None] >= places[None, :]) & (segments[:, None] == segments[None, :])
    return jnp.where(allowed[None], scores, -1e30)


def attend(bundle):
    query_heads, key_heads, value_heads, segments = bundle
    scores = masked_scores(query_heads, key_heads, segments)
    row_max = jnp.max(scores, axis=-1, keepdims=True)
    expo = jnp.exp(scores - row_max)
    row_total = jnp.sum(expo, axis=-1, keepdims=True)
    probability = expo / row_total
    mixed = jnp.einsum(
        "hqk,khd->qhd", rounded(probability), value_heads, preferred_element_type=jnp.float32
    )
    return (rounded(mixed), (row_max + jnp.log(row_total))[..., 0])


def attend_back(bundle):
    query_heads, key_heads, value_heads, segments, log_totals, grad_mixed = bundle
    scores = masked_scores(query_heads, key_heads, segments)
    probability = jnp.exp(scores - log_totals[..., None])
    grad_probs = jnp.einsum(
        "qhd,khd->hqk", grad_mixed, value_heads, preferred_element_type=jnp.float32
    )
    grad_values = jnp.einsum(
        "hqk,qhd->khd", rounded(probability), grad_mixed, preferred_element_type=jnp.float32
    )
    inner_sum = jnp.sum(probability * grad_probs, axis=-1, keepdims=True)
    grad_scores = rounded(probability * (grad_probs - inner_sum))
    grad_queries = jnp.einsum(
        "hqk,khd->qhd", grad_scores, key_heads, preferred_element_type=jnp.float32
    ) * HEAD_DIM ** (-0.5)
    grad_keys = jnp.einsum(
        "hqk,qhd->khd", grad_scores, query_heads, preferred_element_type=jnp.float32
    ) * HEAD_DIM ** (-0.5)
    return (grad_queries, grad_keys, grad_values)


def update(master, moment, average, gradient, rate):
    moment_new = MOMENTUM * moment + gradient
    master_new = master - rate * (gradient + MOMENTUM * moment_new)
    average_new = AVG_DECAY * average + (1.0 - AVG_DECAY) * master_new
    return (master_new, moment_new, average_new)


def on_device(
    input_segments,
    filler_flags,
    sequence_owner,
    prediction_adjoint,
    quadratic_params,
    quadratic_velocity,
    quadratic_mean,
    perceptron_params,
    perceptron_velocity,
    perceptron_mean,
    embedder_params,
    embedder_velocity,
    embedder_mean,
    bias_gain_params,
    bias_gain_velocity,
    bias_gain_mean,
    readout_params,
    readout_velocity,
    readout_mean,
):
    square, ffn, token, vector_low = (
        lax.all_gather(rounded(quadratic_params), ("dp", "head"), axis=1, tiled=True),
        lax.all_gather(rounded(perceptron_params), ("dp", "head"), axis=1, tiled=True),
        lax.all_gather(rounded(embedder_params), ("dp", "head"), axis=1, tiled=True),
        lax.all_gather(rounded(bias_gain_params), ("dp", "head"), axis=1, tiled=True),
    )
    readout_outcome = lax.all_gather(rounded(readout_params), "dp", axis=1, tiled=True)
    vectors = vector_low.astype(jnp.float32)
    tok_count = input_segments.shape[0]
    seq_rows = tok_count // SEQ
    mask_float = filler_flags.astype(jnp.float32)
    tok_input = rounded(jnp.concatenate([input_segments * (1.0 - mask_float), mask_float], axis=1))
    tok_pre = flipped_bilinear(tok_input, token[0]) + vectors[2]
    tok_act = rounded(jax.nn.silu(tok_pre))
    stream_in = (
        matrix_multiply(tok_act, square[0]) + flipped_bilinear(tok_input, token[1]) + vectors[3]
    )
    normed_one, norm_pull_one = jax.vjp(rms_gain, stream_in, vectors[0])
    normed_attn = rounded(normed_one)
    cosines, sines = rope_tables()
    query_heads = rounded(
        rotate(
            matrix_multiply(normed_attn, square[1]).reshape(seq_rows, SEQ, HEADS, HEAD_DIM),
            cosines,
            sines,
        )
    )
    key_heads = rounded(
        rotate(
            matrix_multiply(normed_attn, square[2]).reshape(seq_rows, SEQ, HEADS, HEAD_DIM),
            cosines,
            sines,
        )
    )
    value_heads = rounded(matrix_multiply(normed_attn, square[3])).reshape(
        seq_rows, SEQ, HEADS, HEAD_DIM
    )
    seg_rows = sequence_owner.reshape(seq_rows, SEQ)
    mixed, log_totals = lax.map(attend, (query_heads, key_heads, value_heads, seg_rows))
    attn_mix = mixed.reshape(tok_count, D)
    stream_mid = stream_in + matrix_multiply(attn_mix, square[4])
    normed_two, norm_pull_two = jax.vjp(rms_gain, stream_mid, vectors[1])
    normed_ffn = rounded(normed_two)
    ffn_pre = matrix_multiply(normed_ffn, ffn[0])
    ffn_act = rounded(jax.nn.silu(ffn_pre))
    stream_out = stream_mid + flipped_bilinear(ffn_act, ffn[1])
    stream_low = rounded(stream_out)
    head_pre = matrix_multiply(stream_low, square[5]) + vectors[4]
    head_act = rounded(jax.nn.silu(head_pre))
    shortcut_complete, readout_complete = (
        lax.all_gather(stream_low, "head", axis=0, tiled=True),
        lax.all_gather(head_act, "head", axis=0, tiled=True),
    )
    prediction = (
        matrix_multiply(readout_complete, readout_outcome[0])
        + matrix_multiply(shortcut_complete, readout_outcome[1])
    ).astype(jnp.bfloat16)
    gradient_of_head = jnp.stack(
        [
            bilinear_flipped(readout_complete, prediction_adjoint),
            bilinear_flipped(shortcut_complete, prediction_adjoint),
        ]
    )
    grad_head_act, grad_skip = (
        lax.psum_scatter(
            flipped_bilinear(prediction_adjoint, readout_outcome[0]).astype(jnp.bfloat16),
            "head",
            scatter_dimension=0,
            tiled=True,
        ).astype(jnp.float32),
        lax.psum_scatter(
            flipped_bilinear(prediction_adjoint, readout_outcome[1]).astype(jnp.bfloat16),
            "head",
            scatter_dimension=0,
            tiled=True,
        ).astype(jnp.float32),
    )
    grad_head_pre = rounded(grad_head_act * silu_slope(head_pre))
    grad_bias_head = jnp.sum(grad_head_pre.astype(jnp.float32), axis=0)
    grad_wh = bilinear_flipped(stream_low, grad_head_pre)
    grad_stream_out = grad_skip + flipped_bilinear(grad_head_pre, square[5])
    grad_ffn_out = rounded(grad_stream_out)
    grad_down = bilinear_flipped(grad_ffn_out, ffn_act)
    grad_ffn_pre = rounded(matrix_multiply(grad_ffn_out, ffn[1]) * silu_slope(ffn_pre))
    grad_up = bilinear_flipped(normed_ffn, grad_ffn_pre)
    grad_stream_norm, grad_gain_two = norm_pull_two(flipped_bilinear(grad_ffn_pre, ffn[0]))
    grad_stream_mid = grad_stream_out + grad_stream_norm
    grad_ffn = jnp.stack([grad_up, grad_down])
    grad_attn_out = rounded(grad_stream_mid)
    grad_wo = bilinear_flipped(attn_mix, grad_attn_out)
    grad_attn_mix = rounded(flipped_bilinear(grad_attn_out, square[4])).reshape(
        seq_rows, SEQ, HEADS, HEAD_DIM
    )
    grad_queries, grad_keys, grad_values = lax.map(
        attend_back, (query_heads, key_heads, value_heads, seg_rows, log_totals, grad_attn_mix)
    )
    grad_q_pre = rounded(rotate(grad_queries, cosines, -sines).reshape(tok_count, D))
    grad_k_pre = rounded(rotate(grad_keys, cosines, -sines).reshape(tok_count, D))
    grad_v_pre = rounded(grad_values.reshape(tok_count, D))
    grad_wq = bilinear_flipped(normed_attn, grad_q_pre)
    grad_wk = bilinear_flipped(normed_attn, grad_k_pre)
    grad_wv = bilinear_flipped(normed_attn, grad_v_pre)
    grad_normed = (
        flipped_bilinear(grad_q_pre, square[1])
        + flipped_bilinear(grad_k_pre, square[2])
        + flipped_bilinear(grad_v_pre, square[3])
    )
    grad_stream_first, grad_gain_one = norm_pull_one(grad_normed)
    grad_stream_in = grad_stream_mid + grad_stream_first
    grad_bias_out = jnp.sum(grad_stream_in, axis=0)
    grad_tok_out = rounded(grad_stream_in)
    grad_wb = bilinear_flipped(tok_act, grad_tok_out)
    grad_skip_tok = bilinear_flipped(grad_tok_out, tok_input)
    grad_tok_pre = rounded(flipped_bilinear(grad_tok_out, square[0]) * silu_slope(tok_pre))
    grad_bias_tok = jnp.sum(grad_tok_pre.astype(jnp.float32), axis=0)
    grad_hidden_tok = bilinear_flipped(grad_tok_pre, tok_input)
    grad_input = matrix_multiply(grad_tok_out, token[1]) + matrix_multiply(grad_tok_pre, token[0])
    segment_derivative = grad_input[:, :PATCH] * (1.0 - mask_float)
    grad_square = jnp.stack([grad_wb, grad_wq, grad_wk, grad_wv, grad_wo, grad_wh])
    grad_token = jnp.stack([grad_hidden_tok, grad_skip_tok])
    grad_vector = jnp.stack(
        [grad_gain_one, grad_gain_two, grad_bias_tok, grad_bias_out, grad_bias_head]
    )
    square_share, ffn_share, token_share, vector_share = (
        lax.psum_scatter(grad_square, ("dp", "head"), scatter_dimension=1, tiled=True),
        lax.psum_scatter(grad_ffn, ("dp", "head"), scatter_dimension=1, tiled=True),
        lax.psum_scatter(grad_token, ("dp", "head"), scatter_dimension=1, tiled=True),
        lax.psum_scatter(grad_vector, ("dp", "head"), scatter_dimension=1, tiled=True),
    )
    head_share = lax.psum_scatter(gradient_of_head, "dp", scatter_dimension=1, tiled=True)
    all_tokens = tok_count * lax.axis_size("dp") * lax.axis_size("head")
    matrix_rate = 0.5 / (D * all_tokens) ** 0.5
    quadratic_params_fresh, quadratic_velocity_fresh, quadratic_mean_fresh = update(
        quadratic_params, quadratic_velocity, quadratic_mean, square_share, matrix_rate
    )
    perceptron_params_fresh, perceptron_velocity_fresh, perceptron_mean_fresh = update(
        perceptron_params, perceptron_velocity, perceptron_mean, ffn_share, matrix_rate
    )
    embedder_params_fresh, embedder_velocity_fresh, embedder_mean_fresh = update(
        embedder_params,
        embedder_velocity,
        embedder_mean,
        token_share,
        0.5 / (2 * PATCH * all_tokens) ** 0.5,
    )
    bias_gain_params_fresh, bias_gain_velocity_fresh, bias_gain_mean_fresh = update(
        bias_gain_params, bias_gain_velocity, bias_gain_mean, vector_share, 0.3 / all_tokens**0.5
    )
    readout_params_fresh, readout_velocity_fresh, readout_mean_fresh = update(
        readout_params, readout_velocity, readout_mean, head_share, matrix_rate
    )
    return (
        prediction,
        segment_derivative,
        quadratic_params_fresh,
        quadratic_velocity_fresh,
        quadratic_mean_fresh,
        perceptron_params_fresh,
        perceptron_velocity_fresh,
        perceptron_mean_fresh,
        embedder_params_fresh,
        embedder_velocity_fresh,
        embedder_mean_fresh,
        bias_gain_params_fresh,
        bias_gain_velocity_fresh,
        bias_gain_mean_fresh,
        readout_params_fresh,
        readout_velocity_fresh,
        readout_mean_fresh,
    )


def solution(mesh):
    placed = (
        P(("dp", "head"), None),
        P(("dp", "head"), None),
        P(("dp", "head")),
        P("dp", "head"),
        P(None, ("dp", "head"), None),
        P(None, ("dp", "head"), None),
        P(None, ("dp", "head"), None),
        P(None, ("dp", "head"), None),
        P(None, ("dp", "head"), None),
        P(None, ("dp", "head"), None),
        P(None, ("dp", "head"), None),
        P(None, ("dp", "head"), None),
        P(None, ("dp", "head"), None),
        P(None, ("dp", "head")),
        P(None, ("dp", "head")),
        P(None, ("dp", "head")),
        P(None, "dp", "head"),
        P(None, "dp", "head"),
        P(None, "dp", "head"),
    )
    return jax.shard_map(
        on_device,
        mesh=mesh,
        in_specs=placed,
        out_specs=(
            P("dp", "head"),
            P(("dp", "head"), None),
            P(None, ("dp", "head"), None),
            P(None, ("dp", "head"), None),
            P(None, ("dp", "head"), None),
            P(None, ("dp", "head"), None),
            P(None, ("dp", "head"), None),
            P(None, ("dp", "head"), None),
            P(None, ("dp", "head"), None),
            P(None, ("dp", "head"), None),
            P(None, ("dp", "head"), None),
            P(None, ("dp", "head")),
            P(None, ("dp", "head")),
            P(None, ("dp", "head")),
            P(None, "dp", "head"),
            P(None, "dp", "head"),
            P(None, "dp", "head"),
        ),
        check_vma=False,
    )
```

profile of v0, /device:TPU:1, one launch (start us, length us, event | category | flops | bytes accessed | tf_op | source)
XLA Modules:
  0.0 1786.6 jit_solution(10228850122551237173)
XLA Ops:
  7.3 1.9 convert_element_type.177
  9.2 2.2 convert_element_type.166
  12.6 46.3 %all-gather.13.cloned.1.call-done = bf16[2,1280,320]{2,1,0:T(8,128)(2,1)} async-done(((bf16[2,160,320]{2,1,0:T(8,128)(2,1)}), bf16[2,1280,320]{2,1,0:T(8,128)(2,1)}) %all-gather.13.cloned.1.call-update) | async-done | bytes 1638416 | tf_op jit(solution)/shard_map/all_gather | solution.py:149
  58.9 5.9 convolution_convert_fusion
  65.5 42.5 %all-gather = bf16[32,40,5]{1,2,0:T(8,128)(2,1)S(1)} all-gather(bf16[1,40,5]{1,2,0:T(8,128)(2,1)S(1)} %convert_bitcast_fusion), channel_id=1, replica_groups=mesh['dp'=8,'head'=4] {'dp','head'}, dimensions={0}, use_global_device_ids=true | all-gather | bytes 13200 | tf_op jit(solution)/shard_map/all_gather | solution.py:147
  108.3 41.0 %all_gather.21 = bf16[2,1280,64]{2,1,0:T(8,128)(2,1)S(1)} all-gather(bf16[2,40,64]{2,1,0:T(8,128)(2,1)S(1)} %convert_element_type.162), channel_id=1, replica_groups=mesh['dp'=8,'head'=4] {'dp','head'}, dimensions={1}, use_global_device_ids=true | all-gather | bytes 337920 | tf_op jit(solution)/shard_map/all_gather | solution.py:146
  150.6 2.1 convolution_add_fusion.1
  152.7 5.9 convolution_convert_fusion.1
  158.6 33.8 %all-gather.7.cloned.1.call-done = bf16[6,1280,1280]{2,1,0:T(8,128)(2,1)} async-done(((bf16[6,40,1280]{2,1,0:T(8,128)(2,1)}), bf16[6,1280,1280]{2,1,0:T(8,128)(2,1)}) %all-gather.7.cloned.1.call-update) | async-done | bytes 19660816 | tf_op jit(solution)/shard_map/all_gather | solution.py:144
  192.3 4.9 fusion.23
  197.3 2.1 multiply_reduce_fusion.6
  199.4 6.1 slice_bitcast_fusion.25
  205.5 6.0 copy.104
  211.5 5.6 copy.105
  217.2 2.2 multiply_convert_fusion.6
  219.9 2.0 convolution_bitcast_fusion.13
  221.9 2.0 convolution_bitcast_fusion.12
  224.7 7.7 fusion.58
  232.4 4.8 convolution_convert_fusion.3
  237.3 1.6 copy.103
  238.9 8.8 fusion
  247.7 8.2 fusion.29
  256.0 6.0 multiply_reduce_fusion.5
  262.0 93.0 %all-gather.9.cloned.1.call-done = bf16[2,1280,5120]{2,1,0:T(8,128)(2,1)} async-done(((bf16[2,40,5120]{2,1,0:T(8,128)(2,1)}), bf16[2,1280,5120]{2,1,0:T(8,128)(2,1)}) %all-gather.9.cloned.1.call-update) | async-done | bytes 26214416 | tf_op jit(solution)/shard_map/all_gather | solution.py:145
  355.1 13.3 fusion.3
  368.3 17.6 fusion.22
  385.9 20.5 %reduce-scatter.8.cloned.1.call-done = bf16[512,1280]{1,0:T(8,128)(2,1)} async-done(((bf16[2048,1280]{1,0:T(8,128)(2,1)}), bf16[512,1280]{1,0:T(8,128)(2,1)}) %reduce-scatter.8.cloned.1.call-update) | async-done | bytes 1310736 | tf_op jit(solution)/shard_map/reduce_scatter | solution.py:207
  406.4 7.0 convert_reduce_fusion
  414.3 45.9 %reduce-scatter.6.cloned.1.call-done = bf16[512,1280]{1,0:T(8,128)(2,1)} async-done(((bf16[2048,1280]{1,0:T(8,128)(2,1)}), bf16[512,1280]{1,0:T(8,128)(2,1)}) %reduce-scatter.6.cloned.1.call-update) | async-done | bytes 1310736 | tf_op jit(solution)/shard_map/reduce_scatter | solution.py:213
  460.2 4.2 convolution_add_fusion.4
  465.9 15.5 multiply_convert_fusion.1
  481.4 14.8 multiply_reduce_fusion.1
  496.3 3.2 fusion.27
  500.9 4.9 convolution_convert_fusion.2
  507.5 13.1 multiply_reduce_fusion
  520.6 12.6 multiply_convert_fusion
  533.2 2.6 multiply_bitcast_fusion
  538.4 4.8 fusion.19
  543.2 3.9 convolution_add_fusion.3
  547.2 8.6 fusion.30
  555.8 4.8 multiply_reduce_fusion.2
  562.5 4.3 convert_reduce_fusion.1
  569.8 5.5 convolution_bitcast_fusion.9
  575.3 4.6 convolution_bitcast_fusion.8
  579.9 2.0 pad_maximum_fusion.1
  581.9 7.5 copy.114
  589.5 6.6 fusion.11
  596.1 4.6 fusion.10
  600.7 4.7 fusion.9
  605.4 4.6 fusion.8
  610.0 4.7 fusion.7
  614.6 4.6 fusion.6
  619.5 15.1 convolution_bitcast_fusion.1
  634.6 16.4 convolution_bitcast_fusion
  651.0 35.5 %pad_maximum_fusion = f32[2,1280,5120]{2,1,0:T(8,128)} fusion(f32[1,1280,5120]{2,1,0:T(8,128)} %convolution_bitcast_fusion, f32[1,1280,5120]{2,1,0:T(8,128)} %convolution_bitcast_fusion.1), kind=kLoop, calls=%fused_computation | loop fusion | flops 13107200 | bytes 104857600 | tf_op jit(solution)/shard_map/stack | solution.py:230
  688.5 42.4 %all-reduce.1 = f32[5,1280]{1,0:T(8,128)S(1)} all-reduce(f32[5,1280]{1,0:T(8,128)S(1)} %stack.78), channel_id=7, replica_groups=mesh['dp'=8,'head'=4] {'dp','head'}, use_global_device_ids=true, to_apply=%region_17.18.clone | all-reduce | flops 6400 | bytes 51200
  732.4 1.9 fusion.45
  736.9 4.9 fusion.36
  741.8 5.7 fusion.26
  747.5 106.8 %all-reduce.8.cloned.1.call-done = f32[2,1280,320]{2,0,1:T(2,128)} async-done(((f32[2,1280,320]{2,0,1:T(2,128)}), f32[2,1280,320]{2,0,1:T(2,128)}) %all-reduce.8.cloned.1.call-update) | async-done | bytes 3276816
  856.8 361.0 %reduce-scatter.10.cloned.1.call-done = f32[6,40,1280]{2,1,0:T(8,128)} async-done(((f32[6,1280,1280]{2,1,0:T(8,128)}), f32[6,40,1280]{2,1,0:T(8,128)}) %reduce-scatter.10.cloned.1.call-update) | async-done | bytes 1228816 | tf_op jit(solution)/shard_map/reduce_scatter | solution.py:267
  1217.8 4.6 multiply_add_fusion.4
  1222.3 552.1 %reduce-scatter.12.cloned.1.call-done = f32[2,40,5120]{2,1,0:T(8,128)} async-done(((f32[2,1280,5120]{2,1,0:T(8,128)}), f32[2,40,5120]{2,1,0:T(8,128)}) %reduce-scatter.12.cloned.1.call-update) | async-done | bytes 1638416 | tf_op jit(solution)/shard_map/reduce_scatter | solution.py:268
  1774.4 5.2 multiply_add_fusion
  (209 shorter events, 25.6 us)
Async XLA Ops:
  7.2 51.7 %copy-start = (bf16[2048,320]{0,1:T(8,128)(2,1)S(1)}, bf16[2048,320]{0,1:T(8,128)(2,1)}, u32[]{:S(2)}) copy-start(bf16[2048,320]{0,1:T(8,128)(2,1)} %param.22) | copy-start | bytes 3932164
  7.2 51.7 %all-gather.13.cloned.1.call-start = ((), (), s32[]{:S(2)}) async-start(), calls=%async_computation.7 | async-start | bytes 2211840 | tf_op jit(solution)/shard_map/all_gather | solution.py:149
  9.2 183.2 %all-gather.7.cloned.1.call-start = ((), (), s32[]{:S(2)}) async-start(), calls=%async_computation.4 | async-start | bytes 20275200 | tf_op jit(solution)/shard_map/all_gather | solution.py:144
  11.4 343.6 %all-gather.9.cloned.1.call-start = ((), (), s32[]{:S(2)}) async-start(), calls=%async_computation.5 | async-start | bytes 27033600 | tf_op jit(solution)/shard_map/all_gather | solution.py:145
  12.5 393.9 %reduce-scatter.8.cloned.1.call-start = ((), (), s32[]{:S(2)}) async-start(), calls=%async_computation.10 | async-start | bytes 6553600 | tf_op jit(solution)/shard_map/reduce_scatter | solution.py:207
  64.7 84.5 %copy-start.46 = (s32[512,32]{0,1:T(8,128)S(1)}, s32[512,32]{0,1:T(8,128)}, u32[]{:S(2)}) copy-start(s32[512,32]{0,1:T(8,128)} %param.20) | copy-start | bytes 196612
  64.8 84.6 %copy-start.55 = (f32[512,32]{0,1:T(8,128)S(1)}, f32[512,32]{0,1:T(8,128)}, u32[]{:S(2)}) copy-start(f32[512,32]{0,1:T(8,128)} %param.19) | copy-start | bytes 196612
  64.8 85.6 %copy-start.64 = (s32[512]{0:T(512)S(1)}, s32[512]{0:T(512)}, u32[]{:S(2)}) copy-start(s32[512]{0:T(512)} %param.21) | copy-start | bytes 6148
  64.8 395.4 %reduce-scatter.6.cloned.1.call-start = ((), (), s32[]{:S(2)}) async-start(), calls=%async_computation.9 | async-start | bytes 6553600 | tf_op jit(solution)/shard_map/reduce_scatter | solution.py:213
  108.3 108.9 %copy-start.53 = (f32[1280]{0:T(1024)}, f32[1280]{0:T(1024)S(1)}, u32[]{:S(2)}) copy-start(f32[1280]{0:T(1024)S(1)} %get-tuple-element.125) | copy-start | bytes 15364
  149.3 48.0 %copy-start.11 = (bf16[2,1280,64]{2,1,0:T(8,128)(2,1)}, bf16[2,1280,64]{2,1,0:T(8,128)(2,1)S(1)}, u32[]{:S(2)}) copy-start(bf16[2,1280,64]{2,1,0:T(8,128)(2,1)S(1)} %all_gather.21) | copy-start | bytes 983044
  149.3 48.0 %copy-start.40 = (bf16[512,32]{0,1:T(8,128)(2,1)}, bf16[512,32]{0,1:T(8,128)(2,1)S(1)}, u32[]{:S(2)}) copy-start(bf16[512,32]{0,1:T(8,128)(2,1)S(1)} %convert_convert_fusion) | copy-start | bytes 98308
  149.4 47.9 %copy-start.42 = (bf16[512,32]{0,1:T(8,128)(2,1)}, bf16[512,32]{0,1:T(8,128)(2,1)S(1)}, u32[]{:S(2)}) copy-start(bf16[512,32]{0,1:T(8,128)(2,1)S(1)} %multiply_convert_fusion.8) | copy-start | bytes 98308
  150.4 73.5 %copy-start.44 = (f32[512,40]{0,1:T(8,128)}, f32[512,40]{0,1:T(8,128)S(1)}, u32[]{:S(2)}) copy-start(f32[512,40]{0,1:T(8,128)S(1)} %get-tuple-element.164) | copy-start | bytes 245764
  158.5 411.2 %all-gather.11.cloned.1.call-start = ((), (), s32[]{:S(2)}) async-start(), calls=%async_computation.6 | async-start | bytes 6553600 | tf_op jit(solution)/shard_map/all_gather | solution.py:194
  199.4 6.2 copy-start.58
  199.4 17.8 copy-start.60
  219.3 13.1 copy-start.32
  224.7 7.7 copy-start.17
  224.7 7.7 copy-start.19
  224.7 7.7 copy-start.21
  224.7 7.7 copy-start.23
  238.9 8.8 copy-start.13
  247.7 8.3 copy-start.1
  256.0 6.1 copy-start.9
  385.9 27.5 %copy-start.38 = (bf16[512,1280]{1,0:T(8,128)(2,1)}, bf16[512,1280]{1,0:T(8,128)(2,1)S(1)}, u32[]{:S(2)}) copy-start(bf16[512,1280]{1,0:T(8,128)(2,1)S(1)} %fusion.22) | copy-start | bytes 3932164
  413.4 46.7 %copy-start.70 = (bf16[512,1280]{1,0:T(8,128)(2,1)S(1)}, bf16[512,1280]{1,0:T(8,128)(2,1)}, u32[]{:S(2)}) copy-start(bf16[512,1280]{1,0:T(8,128)(2,1)} %get-tuple-element.135) | copy-start | bytes 3932164
  413.5 161.8 %all-gather.15.cloned.1.call-start = ((), (), s32[]{:S(2)}) async-start(), calls=%async_computation.8 | async-start | bytes 6553600 | tf_op jit(solution)/shard_map/all_gather | solution.py:193
  414.2 321.2 %all-reduce.6.cloned.1.call-start = ((), (), s32[]{:S(2)}) async-start(), calls=%async_computation.13 | async-start | bytes 2621440
  465.9 15.5 copy-start.6
  520.6 12.6 copy-start.22
  520.6 12.6 copy-start.24
  538.4 4.8 copy-start.36
  538.4 4.8 copy-start.34
  547.2 8.6 copy-start.2
  547.2 8.6 copy-start.54
  547.2 8.6 copy-start.61
  555.8 4.9 copy-start.30
  555.8 4.9 copy-start.59
  555.8 4.9 copy-start.4
  569.7 284.6 %all-reduce.8.cloned.1.call-start = ((), (), s32[]{:S(2)}) async-start(), calls=%async_computation.14 | async-start | bytes 7864320
  575.3 4.6 copy-start.29
  589.4 628.3 %reduce-scatter.10.cloned.1.call-start = ((), (), s32[]{:S(2)}) async-start(), calls=%async_computation.11 | async-start | bytes 40550400 | tf_op jit(solution)/shard_map/reduce_scatter | solution.py:267
  589.5 6.6 copy-start.33
  589.5 6.6 copy-start.37
  596.1 4.7 copy-start.35
  600.7 4.7 copy-start.31
  605.4 4.6 copy-start.10
  610.0 4.7 copy-start.39
  610.0 4.7 copy-start.71
  619.3 1155.2 %reduce-scatter.12.cloned.1.call-start = ((), (), s32[]{:S(2)}) async-start(), calls=%async_computation.12 | async-start | bytes 54067200 | tf_op jit(solution)/shard_map/reduce_scatter | solution.py:268
  619.5 15.1 copy-start.27
  686.5 44.4 %copy-start.63 = (f32[5,40]{1,0:T(8,128)S(1)}, f32[5,40]{1,0:T(8,128)}, u32[]{:S(2)}) copy-start(f32[5,40]{1,0:T(8,128)} %param.32) | copy-start | bytes 2404
  686.5 44.4 %copy-start.67 = (f32[5,40]{1,0:T(8,128)S(1)}, f32[5,40]{1,0:T(8,128)}, u32[]{:S(2)}) copy-start(f32[5,40]{1,0:T(8,128)} %param.34) | copy-start | bytes 2404
  686.6 45.8 %copy-start.12 = (bf16[2,1280,64]{2,1,0:T(8,128)(2,1)S(1)}, bf16[2,1280,64]{2,1,0:T(8,128)(2,1)}, u32[]{:S(2)}) copy-start(bf16[2,1280,64]{2,1,0:T(8,128)(2,1)} %copy-done.11) | copy-start | bytes 983044
  686.6 48.2 %copy-start.47 = (s32[512,32]{0,1:T(8,128)S(1)}, s32[512,32]{0,1:T(8,128)}, u32[]{:S(2)}) copy-start(s32[512,32]{0,1:T(8,128)} %param.20) | copy-start | bytes 196612
  686.6 49.6 %copy-start.52 = (f32[2,40,64]{2,1,0:T(8,128)S(1)}, f32[2,40,64]{2,1,0:T(8,128)}, u32[]{:S(2)}) copy-start(f32[2,40,64]{2,1,0:T(8,128)} %param.29) | copy-start | bytes 61444
  686.6 49.6 %copy-start.56 = (f32[2,40,64]{2,1,0:T(8,128)S(1)}, f32[2,40,64]{2,1,0:T(8,128)}, u32[]{:S(2)}) copy-start(f32[2,40,64]{2,1,0:T(8,128)} %param.31) | copy-start | bytes 61444
  686.6 49.6 %copy-start.57 = (f32[2,40,64]{2,1,0:T(8,128)S(1)}, f32[2,40,64]{2,1,0:T(8,128)}, u32[]{:S(2)}) copy-start(f32[2,40,64]{2,1,0:T(8,128)} %param.30) | copy-start | bytes 61444
  736.9 4.9 copy-start.68
  741.8 113.8 %copy-start.28 = (f32[2,160,320]{2,1,0:T(8,128)S(1)}, f32[2,160,320]{2,1,0:T(8,128)}, u32[]{:S(2)}) copy-start(f32[2,160,320]{2,1,0:T(8,128)} %param.35) | copy-start | bytes 1228804
  741.8 113.8 %copy-start.48 = (f32[2,160,320]{2,1,0:T(8,128)S(1)}, f32[2,160,320]{2,1,0:T(8,128)}, u32[]{:S(2)}) copy-start(f32[2,160,320]{2,1,0:T(8,128)} %param.37) | copy-start | bytes 1228804
  741.8 113.8 %copy-start.49 = (f32[2,160,320]{2,1,0:T(8,128)S(1)}, f32[2,160,320]{2,1,0:T(8,128)}, u32[]{:S(2)}) copy-start(f32[2,160,320]{2,1,0:T(8,128)} %param.36) | copy-start | bytes 1228804
  856.8 917.6 %copy-start.8 = (f32[2,40,5120]{2,1,0:T(8,128)S(1)}, f32[2,40,5120]{2,1,0:T(8,128)}, u32[]{:S(2)}) copy-start(f32[2,40,5120]{2,1,0:T(8,128)} %param.26) | copy-start | bytes 4915204
  (19 other events, 35.2 us)
Sparse Core Ops, SparseCore 0:
  10.8 48.0 all-gather.12
  62.3 129.9 all-gather.6
  195.8 159.1 all-gather.8
  357.4 48.9 reduce-scatter.7
  408.8 51.3 reduce-scatter.5
  462.1 40.9 all-gather.10
  505.3 40.3 all-gather.14
  569.8 131.4 all-reduce.5
  704.9 149.3 all-reduce.7
  860.6 357.1 reduce-scatter.9
  1220.1 554.3 reduce-scatter.11
where the time goes:
time: 1790 us
  waiting for transfers between devices  1260 us (70%)
  matrix products  257 us (14%)
  blocking collectives  126 us (7%)
  other arithmetic  87.1 us (5%)
  local copies, waits for them, and re-layouts  39.3 us (2%)
    reduce_scatter x1, waiting for transfers between devices, on_device(): lax.psum_scatter(grad_ffn, ('dp', 'head'), scatter_dimension=1, tiled=True)  552 us
    reduce_scatter x1, waiting for transfers between devices, on_device(): lax.psum_scatter(grad_square, ('dp', 'head'), scatter_dimension=1, tiled=...  361 us
    unnamed x13, waiting for transfers between devices  108 us
    all_gather x1, waiting for transfers between devices, on_device(): lax.all_gather(rounded(perceptron_params), ('dp', 'head'), axis=1, tiled=...  93 us
    dot_general x12, matrix products, flipped_bilinear(): lax.dot_general(left_mat, right_mat, (((1,), (1,)), ((), ())), preferred_...  75.2 us
    dot_general x12, matrix products, bilinear_flipped(): lax.dot_general(left_mat, right_mat, (((0,), (0,)), ((), ())), preferred_...  72 us
    dot_general x12, matrix products, matrix_multiply(): return jnp.dot(left_mat, right_mat, preferred_element_type=jnp.float32)  68.5 us
    all_gather x1, waiting for transfers between devices, on_device(): lax.all_gather(rounded(readout_params), 'dp', axis=1, tiled=True)  46.3 us
  transfers between devices with their start and end apart: 11, of which 8 were waited for; matrix products, arithmetic and copies ran while one was open for 21% of the time, Pallas kernels for 0%

commit v1 on v0

--- a/solution.py
+++ b/solution.py
@@ -146,7 +146,24 @@
         lax.all_gather(rounded(embedder_params), ("dp", "head"), axis=1, tiled=True),
         lax.all_gather(rounded(bias_gain_params), ("dp", "head"), axis=1, tiled=True),
     )
-    readout_outcome = lax.all_gather(rounded(readout_params), "dp", axis=1, tiled=True)
+    x = rounded(readout_params)
+    size, here, extent = (lax.axis_size("dp"), lax.axis_index("dp"), x.shape[1])
+    right = [(i, (i + 1) % size) for i in range(size)]
+    behind = [(i, (i - 1) % size) for i in range(size)]
+    readout_outcome = jnp.zeros((*x.shape[:1], size * extent, *x.shape[1 + 1 :]), x.dtype)
+    readout_outcome = lax.dynamic_update_slice_in_dim(readout_outcome, x, here * extent, axis=1)
+    from_left = from_right = x
+    middle = size // 2
+    for step in range(1, middle + 1):
+        from_left = lax.ppermute(from_left, "dp", right)
+        readout_outcome = lax.dynamic_update_slice_in_dim(
+            readout_outcome, from_left, (here - step) % size * extent, axis=1
+        )
+        if step < size - middle:
+            from_right = lax.ppermute(from_right, "dp", behind)
+            readout_outcome = lax.dynamic_update_slice_in_dim(
+                readout_outcome, from_right, (here + step) % size * extent, axis=1
+            )
     vectors = vector_low.astype(jnp.float32)
     tok_count = input_segments.shape[0]
     seq_rows = tok_count // SEQ

time: 1790 us -> 1710 us (0.955)
  waiting for transfers between devices: 1260 us -> 1140 us
    all_gather x1 -> x0, waiting for transfers between devices: 46.3 us -> none  [on_device(): lax.all_gather(rounded(readout_params), 'dp', axis=1, tiled=True)]
    reduce_scatter x1, waiting for transfers between devices: 45.9 us -> 0.01 us  [on_device(): lax.psum_scatter(flipped_bilinear(prediction_adjoint, readout_outcome[1])...]
    ppermute x0 -> x7, waiting for transfers between devices: none -> 34.1 us  [the longest x4 34.1 us: on_device(): from_left = lax.ppermute(from_left, 'dp', right)]
    all_gather x1, waiting for transfers between devices: 33.8 us -> 0.02 us  [on_device(): lax.all_gather(rounded(quadratic_params), ('dp', 'head'), axis=1, tiled=T...]
    reduce_scatter x1, waiting for transfers between devices: 20.5 us -> 0.01 us  [on_device(): lax.psum_scatter(flipped_bilinear(prediction_adjoint, readout_outcome[0])...]
    unnamed x13 -> x12, waiting for transfers between devices: 108 us -> 106 us
  transfers between devices with their start and end apart: 11 -> 17, of which waited for: 8 -> 8; matrix products, arithmetic and copies ran while one was open for 21% -> 22% of each run, Pallas kernels for 0% -> 0%
where the time goes in v1:
time: 1710 us; the launch traced here: 1700 us
  waiting for transfers between devices  1140 us (67%)
  matrix products  260 us (15%)
  blocking collectives  126 us (7%)
  other arithmetic  89 us (5%)
  local copies, waits for them, and re-layouts  49.3 us (3%)
  starting transfers between devices  18.4 us (1%)
  between operations  18 us (1%)
    reduce_scatter x1, waiting for transfers between devices, on_device(): lax.psum_scatter(grad_ffn, ('dp', 'head'), scatter_dimension=1, tiled=True)  552 us
    reduce_scatter x1, waiting for transfers between devices, on_device(): lax.psum_scatter(grad_square, ('dp', 'head'), scatter_dimension=1, tiled=...  361 us
    unnamed x12, waiting for transfers between devices  106 us
    all_gather x1, waiting for transfers between devices, on_device(): lax.all_gather(rounded(perceptron_params), ('dp', 'head'), axis=1, tiled=...  86.7 us
    dot_general x12, matrix products, flipped_bilinear(): lax.dot_general(left_mat, right_mat, (((1,), (1,)), ((), ())), preferred_...  74 us
    dot_general x12, matrix products, matrix_multiply(): return jnp.dot(left_mat, right_mat, preferred_element_type=jnp.float32)  73.3 us
    dot_general x12, matrix products, bilinear_flipped(): lax.dot_general(left_mat, right_mat, (((0,), (0,)), ((), ())), preferred_...  72 us
    all_gather x1, blocking collectives, on_device(): lax.all_gather(rounded(bias_gain_params), ('dp', 'head'), axis=1, tiled=T...  44.6 us
  transfers between devices with their start and end apart: 17, of which 8 were waited for; matrix products, arithmetic and copies ran while one was open for 22% of the time, Pallas kernels for 0%

profile of v1, /device:TPU:1, one launch (start us, length us, event | category | flops | bytes accessed | tf_op | source)
XLA Modules:
  0.0 1701.1 jit_solution(16208926462721517744)
XLA Ops:
  8.1 2.3 convert_element_type.172
  13.1 2.0 collective-permute-start
  15.1 3.0 collective-permute-start.1
  18.2 8.0 collective-permute-done
  26.2 2.3 collective-permute-start.2
  28.5 3.9 collective-permute-start.3
  33.8 8.3 collective-permute-done.2
  42.1 4.2 collective-permute-start.5
  47.8 6.7 collective-permute-done.4
  54.5 2.3 collective-permute-start.6
  58.2 11.1 collective-permute-done.6
  70.0 5.9 fusion.17
  76.7 44.6 %all-gather = bf16[32,40,5]{1,2,0:T(8,128)(2,1)S(1)} all-gather(bf16[1,40,5]{1,2,0:T(8,128)(2,1)S(1)} %convert_bitcast_fusion), channel_id=1, replica_groups=mesh['dp'=8,'head'=4] {'dp','head'}, dimensions={0}, use_global_device_ids=true | all-gather | bytes 13200 | tf_op jit(solution)/shard_map/all_gather | solution.py:147
  121.5 41.7 %all_gather.18 = bf16[2,1280,64]{2,1,0:T(8,128)(2,1)S(1)} all-gather(bf16[2,40,64]{2,1,0:T(8,128)(2,1)S(1)} %convert_element_type.168), channel_id=1, replica_groups=mesh['dp'=8,'head'=4] {'dp','head'}, dimensions={1}, use_global_device_ids=true | all-gather | bytes 337920 | tf_op jit(solution)/shard_map/all_gather | solution.py:146
  166.5 5.9 fusion.16
  172.5 5.3 fusion.25
  181.3 5.4 convolution_convert_fusion.3
  188.5 6.7 slice_bitcast_fusion.25
  195.2 5.8 copy.110
  201.0 5.8 convolution_bitcast_fusion.13
  206.8 5.6 copy.111
  212.4 4.4 convolution_bitcast_fusion.12
  217.7 7.5 fusion.60
  225.2 8.3 fusion
  233.6 8.3 fusion.31
  241.9 5.9 multiply_reduce_fusion.5
  247.8 86.7 %all-gather.8.cloned.1.call-done = bf16[2,1280,5120]{2,1,0:T(8,128)(2,1)} async-done(((bf16[2,40,5120]{2,1,0:T(8,128)(2,1)}), bf16[2,1280,5120]{2,1,0:T(8,128)(2,1)}) %all-gather.8.cloned.1.call-update) | async-done | bytes 26214416 | tf_op jit(solution)/shard_map/all_gather | solution.py:145
  334.5 13.1 fusion.3
  347.7 17.8 %fusion.24 = bf16[512,1280]{1,0:T(8,128)(2,1)} fusion(f32[512,1280]{1,0:T(8,128)} %get-tuple-element.172, bf16[2,1280,5120]{2,1,0:T(8,128)(2,1)} %all-gather.8.cloned.1.call-done, f32[512,5120]{1,0:T(8,128)} %fusion.3), kind=kOutput, calls=%fused_computation.62 | convolution fusion | flops 6725304320 | bytes 27525120 | tf_op jit(solution)/shard_map/dot_general | solution.py:21
  365.6 5.7 convolution_add_fusion.5
  371.3 5.6 convert_reduce_fusion
  377.9 4.2 convolution_add_fusion.4
  383.6 14.7 multiply_convert_fusion.1
  398.3 14.9 multiply_reduce_fusion.1
  413.3 3.1 fusion.29
  417.9 4.9 convolution_convert_fusion.2
  424.5 12.8 multiply_reduce_fusion
  437.3 12.6 multiply_convert_fusion
  449.9 2.6 multiply_bitcast_fusion
  455.1 4.8 fusion.21
  459.9 3.8 convolution_add_fusion.3
  463.8 8.6 fusion.32
  472.5 4.8 multiply_reduce_fusion.2
  479.1 4.3 convert_reduce_fusion.1
  486.4 5.5 convolution_bitcast_fusion.8
  491.9 4.5 convolution_bitcast_fusion.9
  498.4 7.5 copy.122
  506.0 6.6 fusion.11
  512.6 4.6 fusion.10
  517.3 4.7 fusion.9
  521.9 4.6 fusion.8
  526.5 4.7 fusion.7
  531.2 4.6 fusion.6
  536.1 15.0 convolution_bitcast_fusion.1
  551.1 16.4 convolution_bitcast_fusion
  567.6 35.9 %pad_maximum_fusion = f32[2,1280,5120]{2,1,0:T(8,128)} fusion(f32[1,1280,5120]{2,1,0:T(8,128)} %convolution_bitcast_fusion, f32[1,1280,5120]{2,1,0:T(8,128)} %convolution_bitcast_fusion.1), kind=kLoop, calls=%fused_computation | loop fusion | flops 13107200 | bytes 104857600 | tf_op jit(solution)/shard_map/stack | solution.py:247
  605.5 40.0 %all-reduce.1 = f32[5,1280]{1,0:T(8,128)S(1)} all-reduce(f32[5,1280]{1,0:T(8,128)S(1)} %stack.78), channel_id=7, replica_groups=mesh['dp'=8,'head'=4] {'dp','head'}, use_global_device_ids=true, to_apply=%region_17.18.clone | all-reduce | flops 6400 | bytes 51200
  651.4 4.9 fusion.38
  656.4 5.7 fusion.28
  662.0 105.9 %all-reduce.8.cloned.1.call-done = f32[2,1280,320]{2,0,1:T(2,128)} async-done(((f32[2,1280,320]{2,0,1:T(2,128)}), f32[2,1280,320]{2,0,1:T(2,128)}) %all-reduce.8.cloned.1.call-update) | async-done | bytes 3276816
  770.4 361.0 %reduce-scatter.10.cloned.1.call-done = f32[6,40,1280]{2,1,0:T(8,128)} async-done(((f32[6,1280,1280]{2,1,0:T(8,128)}), f32[6,40,1280]{2,1,0:T(8,128)}) %reduce-scatter.10.cloned.1.call-update) | async-done | bytes 1228816 | tf_op jit(solution)/shard_map/reduce_scatter | solution.py:284
  1131.4 4.6 multiply_add_fusion.4
  1136.0 552.0 %reduce-scatter.12.cloned.1.call-done = f32[2,40,5120]{2,1,0:T(8,128)} async-done(((f32[2,1280,5120]{2,1,0:T(8,128)}), f32[2,40,5120]{2,1,0:T(8,128)}) %reduce-scatter.12.cloned.1.call-update) | async-done | bytes 1638416 | tf_op jit(solution)/shard_map/reduce_scatter | solution.py:285
  1687.9 5.2 multiply_add_fusion
  (231 shorter events, 43.0 us)
Async XLA Ops:
  8.0 62.0 %copy-start = (bf16[2048,320]{0,1:T(8,128)(2,1)S(1)}, bf16[2048,320]{0,1:T(8,128)(2,1)}, u32[]{:S(2)}) copy-start(bf16[2048,320]{0,1:T(8,128)(2,1)} %param.22) | copy-start | bytes 3932164
  8.0 164.4 %all-gather.6.cloned.1.call-start = ((), (), s32[]{:S(2)}) async-start(), calls=%async_computation.4 | async-start | bytes 20275200 | tf_op jit(solution)/shard_map/all_gather | solution.py:144
  10.5 324.1 %all-gather.8.cloned.1.call-start = ((), (), s32[]{:S(2)}) async-start(), calls=%async_computation.5 | async-start | bytes 27033600 | tf_op jit(solution)/shard_map/all_gather | solution.py:145
  11.5 359.7 %reduce-scatter.8.cloned.1.call-start = ((), (), s32[]{:S(2)}) async-start(), calls=%async_computation.9 | async-start | bytes 6553600 | tf_op jit(solution)/shard_map/reduce_scatter | solution.py:224
  13.1 13.1 collective-permute-start
  15.1 13.4 collective-permute-start.1
  26.2 16.0 collective-permute-start.2
  28.5 13.7 collective-permute-start.3
  42.1 12.3 collective-permute-start.4
  42.1 15.4 collective-permute-start.5
  54.5 14.8 collective-permute-start.6
  75.9 87.3 %copy-start.50 = (s32[512,32]{0,1:T(8,128)S(1)}, s32[512,32]{0,1:T(8,128)}, u32[]{:S(2)}) copy-start(s32[512,32]{0,1:T(8,128)} %param.20) | copy-start | bytes 196612
  75.9 87.3 %copy-start.59 = (f32[512,32]{0,1:T(8,128)S(1)}, f32[512,32]{0,1:T(8,128)}, u32[]{:S(2)}) copy-start(f32[512,32]{0,1:T(8,128)} %param.19) | copy-start | bytes 196612
  75.9 88.4 %copy-start.69 = (s32[512]{0:T(512)S(1)}, s32[512]{0:T(512)}, u32[]{:S(2)}) copy-start(s32[512]{0:T(512)} %param.21) | copy-start | bytes 6148
  75.9 300.9 %reduce-scatter.6.cloned.1.call-start = ((), (), s32[]{:S(2)}) async-start(), calls=%async_computation.8 | async-start | bytes 6553600 | tf_op jit(solution)/shard_map/reduce_scatter | solution.py:230
  121.5 57.1 %copy-start.57 = (f32[1280]{0:T(1024)}, f32[1280]{0:T(1024)S(1)}, u32[]{:S(2)}) copy-start(f32[1280]{0:T(1024)S(1)} %get-tuple-element.125) | copy-start | bytes 15364
  163.2 14.6 copy-start.12
  163.2 14.6 copy-start.44
  163.2 14.5 copy-start.46
  164.3 52.5 %copy-start.48 = (f32[512,40]{0,1:T(8,128)}, f32[512,40]{0,1:T(8,128)S(1)}, u32[]{:S(2)}) copy-start(f32[512,40]{0,1:T(8,128)S(1)} %get-tuple-element.166) | copy-start | bytes 245764
  172.4 314.0 %all-gather.12.cloned.1.call-start = ((), (), s32[]{:S(2)}) async-start(), calls=%async_computation.7 | async-start | bytes 6553600 | tf_op jit(solution)/shard_map/all_gather | solution.py:210
  188.5 45.1 %copy-start.14 = (bf16[512,1280]{0,1:T(8,128)(2,1)}, bf16[512,1280]{0,1:T(8,128)(2,1)S(1)}, u32[]{:S(2)}) copy-start(bf16[512,1280]{0,1:T(8,128)(2,1)S(1)} %copy.109) | copy-start | bytes 3932164
  217.6 7.6 copy-start.16
  217.6 7.6 copy-start.18
  217.7 7.5 copy-start.20
  217.7 7.5 copy-start.22
  233.5 8.3 copy-start.2
  241.9 6.0 copy-start.10
  365.5 126.4 %all-gather.10.cloned.1.call-start = ((), (), s32[]{:S(2)}) async-start(), calls=%async_computation.6 | async-start | bytes 6553600 | tf_op jit(solution)/shard_map/all_gather | solution.py:211
  383.6 14.7 copy-start.7
  424.4 225.5 %all-reduce.6.cloned.1.call-start = ((), (), s32[]{:S(2)}) async-start(), calls=%async_computation.12 | async-start | bytes 2621440
  437.2 12.6 copy-start.21
  437.3 12.6 copy-start.23
  455.1 4.8 copy-start.39
  455.1 4.8 copy-start.37
  463.8 8.6 copy-start.3
  463.8 8.6 copy-start.58
  463.8 8.6 copy-start.66
  472.4 4.9 copy-start.33
  472.4 4.9 copy-start.64
  472.4 4.9 copy-start.5
  486.3 281.6 %all-reduce.8.cloned.1.call-start = ((), (), s32[]{:S(2)}) async-start(), calls=%async_computation.13 | async-start | bytes 7864320
  505.9 625.5 %reduce-scatter.10.cloned.1.call-start = ((), (), s32[]{:S(2)}) async-start(), calls=%async_computation.10 | async-start | bytes 40550400 | tf_op jit(solution)/shard_map/reduce_scatter | solution.py:284
  506.0 6.6 copy-start.36
  506.0 6.6 copy-start.40
  512.6 4.6 copy-start.38
  517.3 4.7 copy-start.34
  521.9 4.6 copy-start.11
  526.5 4.7 copy-start.41
  526.5 4.7 copy-start.43
  535.8 1152.1 %reduce-scatter.12.cloned.1.call-start = ((), (), s32[]{:S(2)}) async-start(), calls=%async_computation.11 | async-start | bytes 54067200 | tf_op jit(solution)/shard_map/reduce_scatter | solution.py:285
  536.1 15.1 copy-start.27
  603.5 42.0 %copy-start.68 = (f32[5,40]{1,0:T(8,128)S(1)}, f32[5,40]{1,0:T(8,128)}, u32[]{:S(2)}) copy-start(f32[5,40]{1,0:T(8,128)} %param.32) | copy-start | bytes 2404
  603.5 42.0 %copy-start.71 = (f32[5,40]{1,0:T(8,128)S(1)}, f32[5,40]{1,0:T(8,128)}, u32[]{:S(2)}) copy-start(f32[5,40]{1,0:T(8,128)} %param.34) | copy-start | bytes 2404
  603.5 43.4 %copy-start.13 = (bf16[2,1280,64]{2,1,0:T(8,128)(2,1)S(1)}, bf16[2,1280,64]{2,1,0:T(8,128)(2,1)}, u32[]{:S(2)}) copy-start(bf16[2,1280,64]{2,1,0:T(8,128)(2,1)} %copy-done.12) | copy-start | bytes 983044
  603.5 45.7 %copy-start.51 = (s32[512,32]{0,1:T(8,128)S(1)}, s32[512,32]{0,1:T(8,128)}, u32[]{:S(2)}) copy-start(s32[512,32]{0,1:T(8,128)} %param.20) | copy-start | bytes 196612
  603.5 47.2 %copy-start.56 = (f32[2,40,64]{2,1,0:T(8,128)S(1)}, f32[2,40,64]{2,1,0:T(8,128)}, u32[]{:S(2)}) copy-start(f32[2,40,64]{2,1,0:T(8,128)} %param.29) | copy-start | bytes 61444
  603.6 47.1 %copy-start.60 = (f32[2,40,64]{2,1,0:T(8,128)S(1)}, f32[2,40,64]{2,1,0:T(8,128)}, u32[]{:S(2)}) copy-start(f32[2,40,64]{2,1,0:T(8,128)} %param.31) | copy-start | bytes 61444
  603.6 47.1 %copy-start.61 = (f32[2,40,64]{2,1,0:T(8,128)S(1)}, f32[2,40,64]{2,1,0:T(8,128)}, u32[]{:S(2)}) copy-start(f32[2,40,64]{2,1,0:T(8,128)} %param.30) | copy-start | bytes 61444
  651.4 5.0 copy-start.31
  656.3 112.8 %copy-start.29 = (f32[2,160,320]{2,1,0:T(8,128)S(1)}, f32[2,160,320]{2,1,0:T(8,128)}, u32[]{:S(2)}) copy-start(f32[2,160,320]{2,1,0:T(8,128)} %param.35) | copy-start | bytes 1228804
  656.4 112.8 %copy-start.52 = (f32[2,160,320]{2,1,0:T(8,128)S(1)}, f32[2,160,320]{2,1,0:T(8,128)}, u32[]{:S(2)}) copy-start(f32[2,160,320]{2,1,0:T(8,128)} %param.37) | copy-start | bytes 1228804
  656.4 112.8 %copy-start.53 = (f32[2,160,320]{2,1,0:T(8,128)S(1)}, f32[2,160,320]{2,1,0:T(8,128)}, u32[]{:S(2)}) copy-start(f32[2,160,320]{2,1,0:T(8,128)} %param.36) | copy-start | bytes 1228804
  770.4 917.5 %copy-start.9 = (f32[2,40,5120]{2,1,0:T(8,128)S(1)}, f32[2,40,5120]{2,1,0:T(8,128)}, u32[]{:S(2)}) copy-start(f32[2,40,5120]{2,1,0:T(8,128)} %param.26) | copy-start | bytes 4915204
  (26 other events, 47.4 us)
Sparse Core Ops, SparseCore 0:
  12.3 149.7 all-gather.5
  165.6 168.8 all-gather.7
  486.4 128.5 all-reduce.5
  618.5 149.4 all-reduce.7
  774.2 357.1 reduce-scatter.9
  1133.6 554.3 reduce-scatter.11
Sparse Core Ops, SparseCore 1:
  76.0 93.1 reduce-scatter.7
  172.5 50.1 reduce-scatter.5
  365.6 38.4 all-gather.11
  424.5 38.4 all-gather.9
